TPU v7x, 32 devices: a whole 2x2x4 slice. The times are simulated.
32 devices in a mesh: expert: 8 (over y, x, core), dp: 4 (over z).
Axes of the slice: x: 2, y: 2, z: 4, core: 2. Of those that a mesh axis runs over, the one named last changes fastest.
Arguments:
- tokens: bfloat16 [4096, 2048], P(('expert', 'dp')), may hold values from -6 to 6
- cotangent: bfloat16 [4096, 2048], P(('expert', 'dp')), may hold values from -6 to 6
- router_probs: float32 [4096, 6], P(('expert', 'dp')), may hold values from 0.1 to 0.6
- routes: int32 [4096, 6], P(('expert', 'dp')), may hold values from 0 to 15, all different within a row; in each aligned block of 128 rows (0 to 127, 128 to 255, ...) at most 60 rows name the same one
- partner: int32 [8], replicated, may hold values from 0 to 7, as said below
- gate_weight: bfloat16 [16, 2048, 768], P('expert'), may hold values from -0.125 to 0.125
- up_weight: bfloat16 [16, 2048, 768], P('expert'), may hold values from -0.125 to 0.125
- down_weight: bfloat16 [16, 768, 2048], P('expert'), may hold values from -0.21875 to 0.21875
Outputs:
- output: bfloat16 [4096, 2048], P(('expert', 'dp'))
- token_grad: bfloat16 [4096, 2048], P(('expert', 'dp'))
- expert_grads: bfloat16 [768, 16, 3, 2048], P('dp', 'expert')
Inputs may be any that keep to these rules, and one draw needn't show every extreme that they name: `routes`: each token names 6 different experts. Within the 128 rows of one device no expert is named by more than 60 rows, a bound that some block reaches of them. partner[j] is j or (j + 4) mod 8, and partner[partner[j]] = j.
All inputs are finite; a program needn't handle non-finite values.
Results may differ from a plain program's by a relative error of at most 0.0095.
Values may be sent and summed in bfloat16 or wider, within the bound.
A program may use at most 192 MiB of HBM per device.

v0:
```python
import jax
import jax.numpy as jnp
from jax import lax
from jax.sharding import PartitionSpec as P


def from_partner(value, axis, distance):
    mask = 2**distance
    pairs = [(source, source ^ mask) for source in range(lax.axis_size(axis))]
    return lax.ppermute(value, axis, pairs)


def forward_rows(rows_in, gate_part, up_part):
    gate_pre = jnp.einsum("necd,edf->necf", rows_in, gate_part, preferred_element_type=jnp.float32)
    up_proj = jnp.einsum("necd,edf->necf", rows_in, up_part, preferred_element_type=jnp.float32)
    sigmoid_gate = jax.nn.sigmoid(gate_pre)
    activated = gate_pre * sigmoid_gate
    hidden = (activated * up_proj).astype(jnp.bfloat16)
    return (gate_pre, up_proj, sigmoid_gate, activated, hidden)


def backward_rows(rows_cot, gate_pre, up_proj, sigmoid_gate, activated, down_part):
    grad_hidden = jnp.einsum(
        "necd,efd->necf", rows_cot, down_part, preferred_element_type=jnp.float32
    )
    grad_gate = (
        grad_hidden * up_proj * sigmoid_gate * (1.0 + gate_pre * (1.0 - sigmoid_gate))
    ).astype(jnp.bfloat16)
    grad_up = (grad_hidden * activated).astype(jnp.bfloat16)
    return (grad_gate, grad_up)


def input_grads(grad_gate, grad_up, gate_weight, up_weight):
    summed = jnp.einsum(
        "necf,edf->necd", grad_gate, gate_weight, preferred_element_type=jnp.float32
    )
    summed = summed + jnp.einsum(
        "necf,edf->necd", grad_up, up_weight, preferred_element_type=jnp.float32
    )
    return summed.astype(jnp.bfloat16)


def local(tokens, cotangent, router_probs, routes, partner, gate_weight, up_weight, down_weight):
    tok_dev = tokens.shape[0]
    model_width = tokens.shape[1]
    top_count = routes.shape[1]
    exp_dev = gate_weight.shape[0]
    hidden_units = gate_weight.shape[2]
    owners = lax.axis_size("expert")
    slot_total = exp_dev * owners
    capacity = max(2, 5 * tok_dev * top_count // (4 * slot_total))
    assigned = tok_dev * top_count
    flat_routes = routes.reshape(-1)
    blocks = flat_routes // exp_dev
    owner_ids = jnp.arange(owners, dtype=jnp.int32)
    target = jnp.sum(jnp.where(blocks[:, None] == owner_ids[None, :], partner[None, :], 0), axis=1)
    slot_key = target * exp_dev + flat_routes % exp_dev
    onehot = (slot_key[:, None] == jnp.arange(slot_total, dtype=jnp.int32)[None, :]).astype(
        jnp.int32
    )
    slot_rank = jnp.sum((jnp.cumsum(onehot, axis=0) - 1) * onehot, axis=1)
    slot_row = slot_key * capacity + slot_rank
    source = (
        jnp.full((slot_total * capacity,), assigned, jnp.int32)
        .at[slot_row]
        .set(jnp.arange(assigned, dtype=jnp.int32))
    )
    tok_index = source // top_count
    zero_row = jnp.zeros((1, model_width), jnp.bfloat16)
    padded_tokens = jnp.concatenate([tokens, zero_row], axis=0)
    padded_cot = jnp.concatenate([cotangent, zero_row], axis=0)
    padded_probs = jnp.concatenate([router_probs.reshape(-1), jnp.zeros((1,), jnp.float32)])
    send_tokens = padded_tokens[tok_index].reshape(owners, exp_dev, capacity, model_width)
    send_cot = (padded_probs[source][:, None] * padded_cot[tok_index].astype(jnp.float32)).astype(
        jnp.bfloat16
    )
    send_cot = send_cot.reshape(owners, exp_dev, capacity, model_width)
    recv_tokens, recv_cot = (
        lax.all_to_all(send_tokens, "expert", split_axis=0, concat_axis=0, tiled=True),
        lax.all_to_all(send_cot, "expert", split_axis=0, concat_axis=0, tiled=True),
    )
    gate_pre, up_proj, sigmoid_gate, activated, hidden = forward_rows(
        recv_tokens, gate_weight, up_weight
    )
    expert_out = jnp.einsum(
        "necf,efd->necd", hidden, down_weight, preferred_element_type=jnp.float32
    ).astype(jnp.bfloat16)
    grad_gate, grad_up = backward_rows(
        recv_cot, gate_pre, up_proj, sigmoid_gate, activated, down_weight
    )
    expert_dx = input_grads(grad_gate, grad_up, gate_weight, up_weight)
    back_out, back_dx = (
        lax.all_to_all(expert_out, "expert", split_axis=0, concat_axis=0, tiled=True),
        lax.all_to_all(expert_dx, "expert", split_axis=0, concat_axis=0, tiled=True),
    )
    picked_out = back_out.reshape(slot_total * capacity, model_width)[slot_row].reshape(
        tok_dev, top_count, model_width
    )
    picked_dx = back_dx.reshape(slot_total * capacity, model_width)[slot_row].reshape(
        tok_dev, top_count, model_width
    )
    output = jnp.sum(router_probs[:, :, None] * picked_out.astype(jnp.float32), axis=1).astype(
        jnp.bfloat16
    )
    token_grad = jnp.sum(picked_dx.astype(jnp.float32), axis=1).astype(jnp.bfloat16)
    quarter = hidden_units // lax.axis_size("dp")
    offset = lax.axis_index("dp") * quarter
    gate_part = lax.dynamic_slice_in_dim(gate_weight, offset, quarter, 2)
    up_part = lax.dynamic_slice_in_dim(up_weight, offset, quarter, 2)
    down_part = lax.dynamic_slice_in_dim(down_weight, offset, quarter, 1)
    rows_in = lax.all_gather(recv_tokens, "dp", axis=0, tiled=True)
    rows_cot = lax.all_gather(recv_cot, "dp", axis=0, tiled=True)
    shards = rows_in.shape[0] // owners
    part_gate, part_up, part_sigmoid, part_active, part_hidden = forward_rows(
        rows_in, gate_part, up_part
    )
    part_dgate, part_dup = backward_rows(
        rows_cot, part_gate, part_up, part_sigmoid, part_active, down_part
    )
    split_in = rows_in.reshape(shards, owners, exp_dev, capacity, model_width)
    split_cot = rows_cot.reshape(shards, owners, exp_dev, capacity, model_width)
    split_dgate = part_dgate.reshape(shards, owners, exp_dev, capacity, quarter)
    split_dup = part_dup.reshape(shards, owners, exp_dev, capacity, quarter)
    split_hidden = part_hidden.reshape(shards, owners, exp_dev, capacity, quarter)
    stacked = jnp.stack(
        [
            jnp.einsum(
                "snecf,snecd->sfed", split_dgate, split_in, preferred_element_type=jnp.float32
            ),
            jnp.einsum(
                "snecf,snecd->sfed", split_dup, split_in, preferred_element_type=jnp.float32
            ),
            jnp.einsum(
                "snecf,snecd->sfed", split_hidden, split_cot, preferred_element_type=jnp.float32
            ),
        ],
        axis=3,
    )
    rounded = lax.optimization_barrier(stacked.astype(jnp.bfloat16))
    summed = jnp.sum(rounded.astype(jnp.float32), axis=0)
    rounded_sum = summed.astype(jnp.bfloat16)
    row_here = lax.axis_index("expert")
    partner_here = jnp.sum(jnp.where(owner_ids == row_here, partner, 0))
    swap_bit = owners.bit_length() - 2
    swapped = from_partner(rounded_sum, "expert", swap_bit)
    expert_grads = jnp.where(partner_here == row_here, rounded_sum, swapped)
    return (output, token_grad, expert_grads)


def solution(mesh):
    placed = (
        P(("expert", "dp"), None),
        P(("expert", "dp"), None),
        P(("expert", "dp"), None),
        P(("expert", "dp"), None),
        P(),
        P("expert", None, None),
        P("expert", None, None),
        P("expert", None, None),
    )
    return jax.shard_map(
        local,
        mesh=mesh,
        in_specs=placed,
        out_specs=(
            P(("expert", "dp"), None),
            P(("expert", "dp"), None),
            P("dp", "expert", None, None),
        ),
        check_vma=False,
    )
```

profile of v0, /device:TPU:1, one launch (start us, length us, event | category | flops | bytes accessed | tf_op | source)
XLA Modules:
  0.0 951.5 jit_solution(2456945851649299749)
XLA Ops:
  11.4 3.4 scatter_custom_fusion
  15.9 6.0 gather_fusion
  21.9 4.9 reshape.206
  26.7 6.2 copy.70
  33.0 50.0 %all_to_all.20 = bf16[8,2,60,2048]{3,1,2,0:T(2,128)(2,1)S(1)} all-to-all(bf16[8,2,60,2048]{3,1,2,0:T(2,128)(2,1)S(1)} %copy.70), channel_id=1, replica_groups=mesh['expert'=8,'dp'=4] {'expert'}, dimensions={0} | all-to-all | bytes 7864320 | tf_op jit(solution)/shard_map/all_to_all | solution.py:79
  83.0 1.8 copy-done
  84.8 3.8 copy.71
  89.1 5.9 gather_fusion.3
  95.0 6.6 reshape.217
  101.8 4.3 gather_fusion.2
  106.2 4.5 multiply_convert_fusion
  110.7 4.1 copy.76
  114.8 48.8 %all_to_all.21 = bf16[8,2,60,2048]{3,1,2,0:T(2,128)(2,1)S(1)} all-to-all(bf16[8,2,60,2048]{3,1,2,0:T(2,128)(2,1)S(1)} %copy.76), channel_id=1, replica_groups=mesh['expert'=8,'dp'=4] {'expert'}, dimensions={0} | all-to-all | bytes 7864320 | tf_op jit(solution)/shard_map/all_to_all | solution.py:80
  163.5 1.9 copy-done.2
  165.5 3.8 copy.77
  169.4 8.1 fusion.11
  177.5 4.0 fusion.15
  183.2 4.1 convert_bitcast_fusion
  187.3 5.9 copy.73
  193.2 5.7 all-to-all-start.1
  198.9 8.4 fusion.17
  209.1 5.7 fusion.9
  214.8 160.9 %all-gather.3.cloned.1.call-done = bf16[32,2,60,2048]{3,2,0,1:T(8,128)(2,1)} async-done(((bf16[8,2,60,2048]{3,2,0,1:T(8,128)(2,1)}), bf16[32,2,60,2048]{3,2,0,1:T(8,128)(2,1)}) %all-gather.3.cloned.1.call-update) | async-done | bytes 15728656 | tf_op jit(solution)/shard_map/all_gather | solution.py:111
  375.7 10.8 %fusion.52 = f32[2,192,32,60]{1,3,2,0:T(8,128)} fusion(bf16[32,2,60,2048]{3,2,0,1:T(8,128)(2,1)} %all-gather.3.cloned.1.call-done, bf16[2,2048,768]{2,1,0:T(8,128)(2,1)} %param.14, s32[]{:T(128)S(6)} %select_n.87), kind=kOutput, calls=%fused_computation.69 | convolution fusion | flops 3019898880 | bytes 21823492 | tf_op jit(solution)/shard_map/necd,edf->necf/dot_general | solution.py:15
  386.5 276.3 %all-gather.5.cloned.1.call-done = bf16[32,2,60,2048]{3,2,0,1:T(8,128)(2,1)} async-done(((bf16[8,2,60,2048]{3,2,0,1:T(8,128)(2,1)}), bf16[32,2,60,2048]{3,2,0,1:T(8,128)(2,1)}) %all-gather.5.cloned.1.call-update) | async-done | bytes 15728656 | tf_op jit(solution)/shard_map/all_gather | solution.py:112
  662.8 12.8 %fusion.62 = f32[2,192,32,60]{1,3,2,0:T(8,128)} fusion(bf16[32,2,60,2048]{3,2,0,1:T(8,128)(2,1)} %all-gather.5.cloned.1.call-done, bf16[2,768,2048]{2,1,0:T(8,128)(2,1)} %param.15, s32[]{:T(128)S(6)} %select_n.87), kind=kOutput, calls=%fused_computation.76 | convolution fusion | flops 3019898880 | bytes 21299204 | tf_op jit(solution)/shard_map/necd,efd->necf/dot_general | solution.py:23
  675.6 13.8 %fusion.33 = (bf16[32,2,60,192]{3,2,0,1:T(8,128)(2,1)}, bf16[32,2,60,192]{3,2,0,1:T(8,128)(2,1)S(1)}, bf16[32,2,60,192]{3,2,0,1:T(8,128)(2,1)}) fusion(f32[2,192,32,60]{1,3,2,0:T(8,128)} %fusion.52, f32[2,192,32,60]{1,3,2,0:T(8,128)} %fusion.62, bf16[32,2,60,2048]{3,2,0,1:T(8,128)(2,1)} %all-gather.3.cloned.1.call-done, bf16[2,2048,768]{2,1,0:T(8,128)(2,1)} %param.13, ...), kind=kOutput, calls=%fused_computation.44 | convolution fusion | flops 3030958080 | bytes 31686660 | tf_op jit(solution)/shard_map/necd,edf->necf/dot_general | solution.py:14
  689.4 9.9 %fusion.7 = bf16[4,192,2,1,2048]{4,1,2,0,3:T(8,128)(2,1)} fusion(bf16[4,8,2,60,2048]{4,3,1,0,2:T(8,128)(2,1)} %bitcast.187, bf16[4,8,2,60,192]{4,3,1,0,2:T(8,128)(2,1)} %bitcast.198), kind=kOutput, calls=%fused_computation.20 | convolution fusion | flops 3023044608 | bytes 23494656 | tf_op jit(solution)/shard_map/snecf,snecd->sfed/dot_general | solution.py:130
  699.3 9.9 %fusion.6 = bf16[4,192,2,1,2048]{4,1,2,0,3:T(8,128)(2,1)} fusion(bf16[4,8,2,60,2048]{4,3,1,0,2:T(8,128)(2,1)} %bitcast.188, bf16[4,8,2,60,192]{4,3,1,0,2:T(8,128)(2,1)} %bitcast.197), kind=kOutput, calls=%fused_computation.19 | convolution fusion | flops 3023044608 | bytes 23494656 | tf_op jit(solution)/shard_map/snecf,snecd->sfed/dot_general | solution.py:127
  709.2 9.4 fusion.8
  718.7 16.0 %pad_maximum_fusion = bf16[4,192,2,3,2048]{4,1,2,0,3:T(8,128)(2,1)} fusion(bf16[4,192,2,1,2048]{4,1,2,0,3:T(8,128)(2,1)} %fusion.8, bf16[4,192,2,1,2048]{4,1,2,0,3:T(8,128)(2,1)} %fusion.7, bf16[4,192,2,1,2048]{4,1,2,0,3:T(8,128)(2,1)} %fusion.6), kind=kLoop, calls=%fused_computation.6 | loop fusion | flops 18874368 | bytes 37748736 | tf_op jit(solution)/shard_map/stack | solution.py:125
  734.7 14.0 %reduce_sum.68 = bf16[192,2,3,2048]{3,0,1,2:T(8,128)(2,1)} reduce(bf16[4,192,2,3,2048]{4,1,2,0,3:T(8,128)(2,1)} %pad_maximum_fusion, bf16[]{:T(256)} %constant.35.clone.1), dimensions={0}, to_apply=%region_8.9 | reduce | flops 7077888 | bytes 23592962 | tf_op jit(solution)/shard_map/reduce_sum | solution.py:140
  749.9 13.2 %fusion.27 = bf16[8,2,60,2048]{3,2,0,1:T(8,128)(2,1)} fusion(f32[2,8,60,2048]{3,2,1,0:T(8,128)} %fusion.9, bf16[2,2048,768]{2,1,0:T(8,128)(2,1)} %param.13, f32[2,8,60,768]{3,2,1,0:T(8,128)} %copy-done.14, f32[2,8,60,768]{3,2,1,0:T(8,128)S(1)} %copy-done.11, f32[2,8,60,768]{3,2,1,0:T(8,128)} %copy-done.12), kind=kOutput, calls=%fused_computation.35 | convolution fusion | flops 3031203840 | bytes 26935296 | tf_op jit(solution)/shard_map/necf,edf->necd/dot_general | solution.py:34
  763.1 8.1 copy.78
  771.2 5.8 all-to-all-start.3
  778.2 5.9 copy.74
  784.1 4.9 reshape.207
  789.0 9.0 gather_fusion.1
  797.9 3.7 reshape.216
  801.7 92.3 %all-to-all-done.3 = bf16[8,2,60,2048]{3,1,2,0:T(2,128)(2,1)} async-done(((bf16[8,2,60,2048]{3,1,2,0:T(2,128)(2,1)}), bf16[8,2,60,2048]{3,1,2,0:T(2,128)(2,1)}, u32[]{:S(2)}, u32[]{:S(2)}) %all-to-all-start.3) | async-done | bytes 3932192 | tf_op jit(solution)/shard_map/all_to_all | solution.py:94
  894.0 5.9 copy.79
  899.9 4.9 reshape.209
  904.8 9.0 gather_fusion.4
  913.8 3.0 reshape.210
  916.8 5.7 reduce_sum.66
  922.6 7.5 multiply_reduce_fusion
  930.1 5.0 broadcast_select_fusion
  935.1 9.4 copy.90
  (80 shorter events, 11.2 us)
Async XLA Ops:
  7.2 368.5 %all-gather.3.cloned.1.call-start = ((), (), s32[]{:S(2)}) async-start(), calls=%async_computation.4 | async-start | bytes 20971520 | tf_op jit(solution)/shard_map/all_gather | solution.py:111
  11.4 3.4 copy-start.6
  83.0 1.9 copy-start
  84.8 4.1 copy-start.8
  84.8 4.2 copy-start.5
  88.7 574.1 %all-gather.5.cloned.1.call-start = ((), (), s32[]{:S(2)}) async-start(), calls=%async_computation.5 | async-start | bytes 20971520 | tf_op jit(solution)/shard_map/all_gather | solution.py:112
  89.0 12.6 %copy-start.3 = (f32[128,6]{1,0:T(8,128)}, f32[128,6]{1,0:T(8,128)S(1)}, u32[]{:S(2)}) copy-start(f32[128,6]{1,0:T(8,128)S(1)} %copy.65) | copy-start | bytes 9220
  163.5 1.9 copy-start.2
  169.3 8.1 slice-start.6
  169.3 8.1 copy-start.1
  169.3 8.1 slice-start.7
  169.3 13.8 %slice-start.4 = ((s8[6291456]{0:T(1024)(128)(4,1)}), s8[4194304]{0:T(1024)(128)(4,1)S(1)}, s32[]{:S(2)}) async-start(s8[6291456]{0:T(1024)(128)(4,1)} %bitcast.192), calls=%async_computation.10 | async-start | bytes 8388608
  177.5 4.1 copy-start.10
  177.5 5.7 slice-start.5
  181.5 1.6 copy-start.12
  193.2 15.9 %slice-start.2 = ((s8[6291456]{0:T(1024)(128)(4,1)}), s8[2097152]{0:T(1024)(128)(4,1)S(1)}, s32[]{:S(2)}) async-start(s8[6291456]{0:T(1024)(128)(4,1)} %bitcast.190), calls=%async_computation.8 | async-start | bytes 4194304
  193.2 578.0 %all-to-all-start.1 = ((bf16[8,2,60,2048]{3,1,2,0:T(2,128)(2,1)}), bf16[8,2,60,2048]{3,1,2,0:T(2,128)(2,1)}, u32[]{:S(2)}, u32[]{:S(2)}) async-start(bf16[8,2,60,2048]{3,1,2,0:T(2,128)(2,1)} %copy.73), calls=%async_computation.1 | async-start | bytes 7864320 | tf_op jit(solution)/shard_map/all_to_all | solution.py:93
  198.9 10.2 %slice-start.3 = ((s8[6291456]{0:T(1024)(128)(4,1)}), s8[4194304]{0:T(1024)(128)(4,1)S(1)}, s32[]{:S(2)}) async-start(s8[6291456]{0:T(1024)(128)(4,1)} %bitcast.190), calls=%async_computation.9 | async-start | bytes 8388608
  198.9 10.2 %copy-start.13 = (f32[2,8,60,768]{3,2,1,0:T(8,128)S(1)}, f32[2,8,60,768]{3,2,1,0:T(8,128)}, u32[]{:S(2)}) copy-start(f32[2,8,60,768]{3,2,1,0:T(8,128)} %copy-done.12) | copy-start | bytes 8847364
  207.3 1.8 copy-start.14
  734.7 15.2 %copy-start.11 = (f32[2,8,60,768]{3,2,1,0:T(8,128)S(1)}, f32[2,8,60,768]{3,2,1,0:T(8,128)}, u32[]{:S(2)}) copy-start(f32[2,8,60,768]{3,2,1,0:T(8,128)} %copy-done.10) | copy-start | bytes 8847364
  748.7 181.5 %collective-permute-start = (bf16[192,2,3,2048]{3,0,1,2:T(8,128)(2,1)}, bf16[192,2,3,2048]{3,0,1,2:T(8,128)(2,1)}, u32[]{:S(2)}, u32[]{:S(2)}) collective-permute-start(bf16[192,2,3,2048]{3,0,1,2:T(8,128)(2,1)} %reduce_sum.68), channel_id=1, source_target_pairs={{0,16},{4,20},{8,24},{12,28},{16,0},{20,4},{24,8},{28,12},{1,17},{... | collective-permute-start | bytes 14155784 | tf_op jit(solution)/shard_map/ppermute | solution.py:10
  771.2 5.8 copy-start.9
  771.2 7.0 copy-start.7
  771.2 122.7 %all-to-all-start.3 = ((bf16[8,2,60,2048]{3,1,2,0:T(2,128)(2,1)}), bf16[8,2,60,2048]{3,1,2,0:T(2,128)(2,1)}, u32[]{:S(2)}, u32[]{:S(2)}) async-start(bf16[8,2,60,2048]{3,1,2,0:T(2,128)(2,1)} %copy.78), calls=%async_computation.3 | async-start | bytes 7864320 | tf_op jit(solution)/shard_map/all_to_all | solution.py:94
  916.8 5.8 copy-start.4
  916.8 13.3 %slice-start = ((s8[4718592]{0:T(1024)(128)(4,1)}), s8[524288]{0:T(1024)(128)(4,1)S(1)}, s32[]{:S(2)}) async-start(s8[4718592]{0:T(1024)(128)(4,1)} %bitcast.184), calls=%async_computation.6 | async-start | bytes 1048576
  922.6 7.6 slice-start.1
Sparse Core Ops, SparseCore 0:
  88.8 286.8 all-gather.2
  377.8 284.9 all-gather.4
where the time goes:
time: 960 us; the launch traced here: 951 us
  waiting for transfers between devices  530 us (55%)
  local copies, waits for them, and re-layouts  129 us (13%)
  matrix products  110 us (11%)
  blocking collectives  98.8 us (10%)
  other arithmetic  56 us (6%)
  between operations  15.2 us (2%)
  starting transfers between devices  12.9 us (1%)
    all_gather x1, waiting for transfers between devices, local(): rows_cot = lax.all_gather(recv_cot, 'dp', axis=0, tiled=True)  276 us
    all_gather x1, waiting for transfers between devices, local(): rows_in = lax.all_gather(recv_tokens, 'dp', axis=0, tiled=True)  161 us
    all_to_all x1, waiting for transfers between devices, local(): lax.all_to_all(expert_dx, 'expert', split_axis=0, concat_axis=0, tiled=True)  92.3 us
    all_to_all x1, blocking collectives, local(): lax.all_to_all(send_tokens, 'expert', split_axis=0, concat_axis=0, tiled=...  50 us
    all_to_all x1, blocking collectives, local(): lax.all_to_all(send_cot, 'expert', split_axis=0, concat_axis=0, tiled=True)  48.8 us
    dot_general x2, matrix products, backward_rows(): jnp.einsum('necd,efd->necf', rows_cot, down_part, preferred_element_type=...  21.2 us
  transfers between devices with their start and end apart: 5, of which 3 were waited for; matrix products, arithmetic and copies ran while one was open for 26% of the time, Pallas kernels for 0%

commit v1 on v0

--- a/solution.py
+++ b/solution.py
@@ -108,8 +108,11 @@
     gate_part = lax.dynamic_slice_in_dim(gate_weight, offset, quarter, 2)
     up_part = lax.dynamic_slice_in_dim(up_weight, offset, quarter, 2)
     down_part = lax.dynamic_slice_in_dim(down_weight, offset, quarter, 1)
-    rows_in = lax.all_gather(recv_tokens, "dp", axis=0, tiled=True)
-    rows_cot = lax.all_gather(recv_cot, "dp", axis=0, tiled=True)
+    rows_in, rows_cot = jnp.split(
+        lax.all_gather(jnp.concatenate([recv_tokens, recv_cot], axis=1), "dp", axis=0, tiled=True),
+        [recv_tokens.shape[1]],
+        axis=1,
+    )
     shards = rows_in.shape[0] // owners
     part_gate, part_up, part_sigmoid, part_active, part_hidden = forward_rows(
         rows_in, gate_part, up_part

time: 960 us -> 1050 us (1.094)
  waiting for transfers between devices: 530 us -> 657 us
  blocking collectives: 98.8 us -> 0 us
  local copies, waits for them, and re-layouts: 129 us -> 154 us
  starting transfers between devices: 12.9 us -> 29.5 us
    all_to_all x2 -> x0, blocking collectives: 98.8 us -> none  [the longest x1 50 us: local(): lax.all_to_all(send_tokens, 'expert', split_axis=0, concat_axis=0, tiled=...]
    all_to_all x1, waiting for transfers between devices: 0.01 us -> 95.8 us  [local(): lax.all_to_all(expert_out, 'expert', split_axis=0, concat_axis=0, tiled=T...]
    all_to_all x1, waiting for transfers between devices: 92.3 us -> 0.01 us  [local(): lax.all_to_all(expert_dx, 'expert', split_axis=0, concat_axis=0, tiled=True)]
    all_gather x2 -> x1, waiting for transfers between devices: 437 us -> 501 us  [local(): lax.all_gather(jnp.concatenate([recv_tokens, recv_cot], axis=1), 'dp', ax...]
    all_to_all x0 -> x2, waiting for transfers between devices: none -> 60.3 us  [the longest x1 36.4 us: local(): lax.all_to_all(send_tokens, 'expert', split_axis=0, concat_axis=0, tiled=...]
    split x0 -> x1, local copies, waits for them, and re-layouts: none -> 23.4 us  [local(): jnp.split(lax.all_gather(jnp.concatenate([recv_tokens, recv_cot], axis=1)...]
    all_to_all x0 -> x2, starting transfers between devices: none -> 13.5 us  [the longest x1 7.9 us: local(): lax.all_to_all(send_tokens, 'expert', split_axis=0, concat_axis=0, tiled=...]
  transfers between devices with their start and end apart: 5 -> 6, of which waited for: 3 -> 4; matrix products, arithmetic and copies ran while one was open for 26% -> 26% of each run, Pallas kernels for 0% -> 0%
where the time goes in v1:
time: 1050 us; the launch traced here: 1040 us
  waiting for transfers between devices  657 us (63%)
  local copies, waits for them, and re-layouts  154 us (15%)
  matrix products  120 us (11%)
  other arithmetic  62.9 us (6%)
  starting transfers between devices  29.5 us (3%)
  between operations  15.4 us (1%)
    all_gather x1, waiting for transfers between devices, local(): lax.all_gather(jnp.concatenate([recv_tokens, recv_cot], axis=1), 'dp', ax...  501 us
    all_to_all x1, waiting for transfers between devices, local(): lax.all_to_all(expert_out, 'expert', split_axis=0, concat_axis=0, tiled=T...  95.8 us
    all_to_all x1, waiting for transfers between devices, local(): lax.all_to_all(send_tokens, 'expert', split_axis=0, concat_axis=0, tiled=...  36.4 us
    all_to_all x1, waiting for transfers between devices, local(): lax.all_to_all(send_cot, 'expert', split_axis=0, concat_axis=0, tiled=True)  23.8 us
    split x1, local copies, waits for them, and re-layouts, local(): jnp.split(lax.all_gather(jnp.concatenate([recv_tokens, recv_cot], axis=1)...  23.4 us
    dot_general x2, matrix products, forward_rows(): jnp.einsum('necd,edf->necf', rows_in, gate_part, preferred_element_type=j...  22.8 us
    dot_general x2, matrix products, backward_rows(): jnp.einsum('necd,efd->necf', rows_cot, down_part, preferred_element_type=...  22.7 us
  transfers between devices with their start and end apart: 6, of which 4 were waited for; matrix products, arithmetic and copies ran while one was open for 26% of the time, Pallas kernels for 0%

profile of v1, /device:TPU:1, one launch (start us, length us, event | category | flops | bytes accessed | tf_op | source)
XLA Modules:
  0.0 1039.0 jit_solution(12501414740318853729)
XLA Ops:
  11.9 3.4 scatter_custom_fusion
  16.4 5.9 gather_fusion.3
  22.3 6.0 reshape.217
  29.2 4.3 gather_fusion.2
  33.6 3.9 multiply_convert_fusion
  37.5 5.9 copy.76
  43.4 5.6 all-to-all-start.2
  49.1 5.9 gather_fusion
  55.0 4.9 reshape.206
  59.9 8.1 copy.70
  68.0 23.8 %all-to-all-done.2 = bf16[8,2,60,2048]{3,1,2,0:T(2,128)(2,1)} async-done(((bf16[8,2,60,2048]{3,1,2,0:T(2,128)(2,1)}), bf16[8,2,60,2048]{3,1,2,0:T(2,128)(2,1)}, u32[]{:S(2)}, u32[]{:S(2)}) %all-to-all-start.2) | async-done | bytes 3932192 | tf_op jit(solution)/shard_map/all_to_all | solution.py:80
  91.9 7.9 all-to-all-start
  100.2 6.0 copy.77
  106.1 36.4 %all-to-all-done = bf16[8,2,60,2048]{3,1,2,0:T(2,128)(2,1)} async-done(((bf16[8,2,60,2048]{3,1,2,0:T(2,128)(2,1)}), bf16[8,2,60,2048]{3,1,2,0:T(2,128)(2,1)}, u32[]{:S(2)}, u32[]{:S(2)}) %all-to-all-start) | async-done | bytes 3932192 | tf_op jit(solution)/shard_map/all_to_all | solution.py:79
  142.6 5.9 copy.71
  148.4 7.5 pad_maximum_fusion.1
  156.0 9.9 fusion.17
  165.9 9.0 fusion.15
  174.9 8.5 fusion.11
  183.5 5.6 fusion.9
  189.1 13.5 %fusion.27 = bf16[8,2,60,2048]{3,2,0,1:T(8,128)(2,1)} fusion(f32[2,8,60,2048]{3,2,1,0:T(8,128)} %fusion.9, bf16[2,2048,768]{2,1,0:T(8,128)(2,1)} %param.13, f32[2,8,60,768]{3,2,1,0:T(8,128)} %fusion.17, f32[2,8,60,768]{3,2,1,0:T(8,128)} %fusion.11, f32[2,8,60,768]{3,2,1,0:T(8,128)S(1)} %copy-done.7), kind=kOutput, calls=%fused_computation.36 | convolution fusion | flops 3031203840 | bytes 26935296 | tf_op jit(solution)/shard_map/necf,edf->necd/dot_general | solution.py:34
  202.6 8.2 copy.78
  210.8 8.8 all-to-all-start.3
  219.6 501.2 %all-gather.2.cloned.1.call-done = bf16[32,4,60,2048]{3,2,0,1:T(8,128)(2,1)} async-done(((bf16[8,4,60,2048]{3,2,0,1:T(8,128)(2,1)}), bf16[32,4,60,2048]{3,2,0,1:T(8,128)(2,1)}) %all-gather.2.cloned.1.call-update) | async-done | bytes 31457296 | tf_op jit(solution)/shard_map/all_gather | solution.py:112
  720.7 10.6 %fusion.52 = f32[2,192,32,60]{1,3,2,0:T(8,128)} fusion(bf16[2,2048,768]{2,1,0:T(8,128)(2,1)} %param.14, s32[]{:T(128)S(6)} %select_n.87, bf16[32,4,60,2048]{3,2,0,1:T(8,128)(2,1)} %all-gather.2.cloned.1.call-done), kind=kOutput, calls=%fused_computation.70 | convolution fusion | flops 3019898880 | bytes 21823492 | tf_op jit(solution)/shard_map/necd,edf->necf/dot_general | solution.py:15
  731.3 12.8 %fusion.62 = f32[2,192,32,60]{1,3,2,0:T(8,128)} fusion(bf16[2,768,2048]{2,1,0:T(8,128)(2,1)} %param.15, s32[]{:T(128)S(6)} %select_n.87, bf16[32,4,60,2048]{3,2,0,1:T(8,128)(2,1)} %all-gather.2.cloned.1.call-done), kind=kOutput, calls=%fused_computation.77 | convolution fusion | flops 3019898880 | bytes 21299204 | tf_op jit(solution)/shard_map/necd,efd->necf/dot_general | solution.py:23
  744.1 23.4 %fusion.93 = (bf16[32,2,60,2048]{3,2,0,1:T(8,128)(2,1)}, bf16[32,2,60,2048]{3,2,0,1:T(8,128)(2,1)}) fusion(bf16[32,4,60,2048]{3,2,0,1:T(8,128)(2,1)} %all-gather.2.cloned.1.call-done), kind=kLoop, calls=%fused_computation.139 | loop fusion | bytes 62914560 | tf_op jit(solution)/shard_map/split | solution.py:111
  767.5 13.8 %fusion.33 = (bf16[32,2,60,192]{3,2,0,1:T(8,128)(2,1)}, bf16[32,2,60,192]{3,2,0,1:T(8,128)(2,1)S(1)}, bf16[32,2,60,192]{3,2,0,1:T(8,128)(2,1)}) fusion(f32[2,192,32,60]{1,3,2,0:T(8,128)} %fusion.52, f32[2,192,32,60]{1,3,2,0:T(8,128)} %fusion.62, bf16[32,4,60,2048]{3,2,0,1:T(8,128)(2,1)} %all-gather.2.cloned.1.call-done, bf16[2,2048,768]{2,1,0:T(8,128)(2,1)} %param.13, ...), kind=kOutput, calls=%fused_computation.45 | convolution fusion | flops 3030958080 | bytes 31686660 | tf_op jit(solution)/shard_map/necd,edf->necf/dot_general | solution.py:14
  781.3 10.4 fusion.6
  791.7 9.9 fusion.7
  801.6 9.2 fusion.8
  810.8 16.0 %pad_maximum_fusion = bf16[4,192,2,3,2048]{4,1,2,0,3:T(8,128)(2,1)} fusion(bf16[4,192,2,1,2048]{4,1,2,0,3:T(8,128)(2,1)} %fusion.8, bf16[4,192,2,1,2048]{4,1,2,0,3:T(8,128)(2,1)} %fusion.7, bf16[4,192,2,1,2048]{4,1,2,0,3:T(8,128)(2,1)} %fusion.6), kind=kLoop, calls=%fused_computation.6 | loop fusion | flops 18874368 | bytes 37748736 | tf_op jit(solution)/shard_map/stack | solution.py:128
  826.9 14.1 %reduce_sum.68 = bf16[192,2,3,2048]{3,0,1,2:T(8,128)(2,1)} reduce(bf16[4,192,2,3,2048]{4,1,2,0,3:T(8,128)(2,1)} %pad_maximum_fusion, bf16[]{:T(256)} %constant.35.clone.1), dimensions={0}, to_apply=%region_8.9 | reduce | flops 7077888 | bytes 23592962 | tf_op jit(solution)/shard_map/reduce_sum | solution.py:143
  842.2 7.2 convert_bitcast_fusion
  849.4 5.9 copy.73
  855.3 5.6 all-to-all-start.1
  862.2 5.9 copy.79
  868.1 4.9 reshape.209
  873.0 9.0 gather_fusion.4
  884.8 5.7 reduce_sum.66
  890.5 95.8 %all-to-all-done.1 = bf16[8,2,60,2048]{3,1,2,0:T(2,128)(2,1)} async-done(((bf16[8,2,60,2048]{3,1,2,0:T(2,128)(2,1)}), bf16[8,2,60,2048]{3,1,2,0:T(2,128)(2,1)}, u32[]{:S(2)}, u32[]{:S(2)}) %all-to-all-start.1) | async-done | bytes 3932192 | tf_op jit(solution)/shard_map/all_to_all | solution.py:93
  986.3 5.9 copy.74
  992.2 4.9 reshape.207
  997.1 9.2 gather_fusion.1
  1006.3 3.7 reshape.216
  1010.0 7.4 multiply_reduce_fusion
  1017.4 4.9 broadcast_select_fusion
  1022.3 9.4 copy.90
  (61 shorter events, 12.0 us)
Async XLA Ops:
  11.3 0.6 copy-start.3
  22.3 6.0 copy-start.5
  28.4 0.6 copy-start
  43.4 5.6 copy-start.2
  43.4 48.4 %all-to-all-start.2 = ((bf16[8,2,60,2048]{3,1,2,0:T(2,128)(2,1)}), bf16[8,2,60,2048]{3,1,2,0:T(2,128)(2,1)}, u32[]{:S(2)}, u32[]{:S(2)}) async-start(bf16[8,2,60,2048]{3,1,2,0:T(2,128)(2,1)} %copy.76), calls=%async_computation.2 | async-start | bytes 7864320 | tf_op jit(solution)/shard_map/all_to_all | solution.py:80
  91.9 50.7 %all-to-all-start = ((bf16[8,2,60,2048]{3,1,2,0:T(2,128)(2,1)}), bf16[8,2,60,2048]{3,1,2,0:T(2,128)(2,1)}, u32[]{:S(2)}, u32[]{:S(2)}) async-start(bf16[8,2,60,2048]{3,1,2,0:T(2,128)(2,1)} %copy.70), calls=%async_computation | async-start | bytes 7864320 | tf_op jit(solution)/shard_map/all_to_all | solution.py:79
  99.8 621.0 %all-gather.2.cloned.1.call-start = ((), (), s32[]{:S(2)}) async-start(), calls=%async_computation.4 | async-start | bytes 41943040 | tf_op jit(solution)/shard_map/all_gather | solution.py:112
  155.9 10.0 slice-start.2
  155.9 10.0 slice-start.3
  156.0 19.0 %slice-start = ((s8[6291456]{0:T(1024)(128)(4,1)}), s8[4194304]{0:T(1024)(128)(4,1)S(1)}, s32[]{:S(2)}) async-start(s8[6291456]{0:T(1024)(128)(4,1)} %bitcast.185), calls=%async_computation.5 | async-start | bytes 8388608
  165.9 9.0 slice-start.1
  174.9 8.6 copy-start.7
  174.9 8.6 copy-start.9
  210.8 644.5 %all-to-all-start.3 = ((bf16[8,2,60,2048]{3,1,2,0:T(2,128)(2,1)}), bf16[8,2,60,2048]{3,1,2,0:T(2,128)(2,1)}, u32[]{:S(2)}, u32[]{:S(2)}) async-start(bf16[8,2,60,2048]{3,1,2,0:T(2,128)(2,1)} %copy.78), calls=%async_computation.3 | async-start | bytes 7864320 | tf_op jit(solution)/shard_map/all_to_all | solution.py:94
  826.9 15.3 %copy-start.8 = (f32[2,8,60,768]{3,2,1,0:T(8,128)S(1)}, f32[2,8,60,768]{3,2,1,0:T(8,128)}, u32[]{:S(2)}) copy-start(f32[2,8,60,768]{3,2,1,0:T(8,128)} %fusion.15) | copy-start | bytes 8847364
  841.0 176.4 %collective-permute-start = (bf16[192,2,3,2048]{3,0,1,2:T(8,128)(2,1)}, bf16[192,2,3,2048]{3,0,1,2:T(8,128)(2,1)}, u32[]{:S(2)}, u32[]{:S(2)}) collective-permute-start(bf16[192,2,3,2048]{3,0,1,2:T(8,128)(2,1)} %reduce_sum.68), channel_id=1, source_target_pairs={{0,16},{4,20},{8,24},{12,28},{16,0},{20,4},{24,8},{28,12},{1,17},{... | collective-permute-start | bytes 14155784 | tf_op jit(solution)/shard_map/ppermute | solution.py:10
  855.3 5.6 copy-start.6
  855.3 6.9 copy-start.4
  855.3 131.0 %all-to-all-start.1 = ((bf16[8,2,60,2048]{3,1,2,0:T(2,128)(2,1)}), bf16[8,2,60,2048]{3,1,2,0:T(2,128)(2,1)}, u32[]{:S(2)}, u32[]{:S(2)}) async-start(bf16[8,2,60,2048]{3,1,2,0:T(2,128)(2,1)} %copy.73), calls=%async_computation.1 | async-start | bytes 7864320 | tf_op jit(solution)/shard_map/all_to_all | solution.py:93
  1006.3 3.7 copy-start.1
Sparse Core Ops, SparseCore 0:
  156.1 564.6 all-gather.1
